TPU v7x, 512 devices: a whole 4x8x8 slice. The times are simulated.
512 devices in a mesh: member: 16 (over z, core), band: 32 (over y, x).
Axes of the slice: x: 4, y: 8, z: 8, core: 2. Of those that a mesh axis runs over, the one named last changes fastest.
Arguments:
- ensemble: bfloat16 [16, 2, 16, 128, 1440], P('member', None, None, 'band'), may hold values from -6 to 6
- member_weight: float32 [16], replicated, may hold values from 0.5 to 2
- member_of_slot: int32 [16], P('member'), may hold values from 0 to 15, each once
- halfwidth: int32 [16], replicated, may hold values from 1 to 4, as said below
- static_root: float32 [16, 16], replicated, may hold values from -1.5 to 1.5
- innovation: bfloat16 [2, 16, 128, 1440], P(None, None, 'band'), may hold values from -6 to 6
- precision: bfloat16 [16, 128, 1440], P(None, 'band'), may hold values from 0.1 to 3
Outputs:
- control_members: float32 [16, 16, 128, 1440], P('member', None, 'band')
- control_static: float32 [16, 128, 1440], P(None, 'band')
- increment: float32 [2, 16, 128, 1440], P(None, 'member', 'band')
Inputs may be any that keep to these rules, and one draw needn't show every extreme that they name: `member_of_slot`: each member appears in exactly one slot. `halfwidth`: some level has a half-width of exactly 4.
All inputs are finite; a program needn't handle non-finite values.
Results may differ from a plain program's by a relative error of at most 0.0062.
Values may be sent and summed in bfloat16 or wider, within the bound.
A program may use at most 64 MiB of HBM per device.

v0:
```python
import math
import jax
import jax.numpy as jnp
from jax import lax
from jax.sharding import PartitionSpec as P

ITERS = 2
HMAX = 4
LREACH = 18
ensemble_share = 0.8
static_share = 0.6
length_scale = 6.0


def with_halo(block, sides, width):
    for axis, dim in sides:
        count = lax.axis_size(axis)
        forward = [(i, i + 1) for i in range(count - 1)]
        backward = [(target, source) for source, target in forward]
        low = lax.ppermute(
            lax.slice_in_dim(block, block.shape[dim] - width, None, axis=dim), axis, forward
        )
        high = lax.ppermute(lax.slice_in_dim(block, 0, width, axis=dim), axis, backward)
        block = jnp.concatenate([low, block, high], axis=dim)
    return block


def lon_kernel(reach, width):
    rows_index = jnp.arange(width + 2 * reach, dtype=jnp.int32)[:, None]
    cols_index = jnp.arange(width, dtype=jnp.int32)[None, :]
    distance = jnp.abs(rows_index - reach - cols_index).astype(jnp.float32)
    values = jnp.exp(-0.5 * (distance / length_scale) ** 2) / (
        length_scale * math.sqrt(2.0 * math.pi)
    )
    return jnp.where(distance <= reach, values, jnp.zeros_like(values)).astype(jnp.bfloat16)


def smooth_longitude(field, reach, blocks):
    width = field.shape[-1] // blocks
    pieces = field.reshape(field.shape[:-1] + (blocks, width))
    before = jnp.roll(pieces, 1, axis=-2)[..., width - reach :]
    after = jnp.roll(pieces, -1, axis=-2)[..., :reach]
    window = jnp.concatenate([before, pieces, after], axis=-1)
    kernel = lon_kernel(reach, width)
    result = jnp.einsum("...bm,mo->...bo", window, kernel, preferred_element_type=jnp.float32)
    return result.reshape(field.shape).astype(jnp.bfloat16)


def taper_weights(halfwidth, reach):
    offsets = jnp.abs(jnp.arange(-reach, reach + 1, dtype=jnp.int32)).astype(jnp.float32)
    spans = halfwidth.astype(jnp.float32)[:, None] + 1.0
    return jnp.maximum(1.0 - offsets[None, :] / spans, 0.0) / spans


def localize(field, taper):
    smoothed = smooth_longitude(field.astype(jnp.bfloat16), LREACH, 3)
    padded = with_halo(smoothed, (("band", 2),), HMAX)
    row_count = field.shape[2]
    summed = jnp.zeros(field.shape, jnp.float32)
    for offset in range(2 * HMAX + 1):
        summed = summed + taper[:, offset][None, :, None, None] * padded[
            :, :, offset : offset + row_count, :
        ].astype(jnp.float32)
    return summed


def local_dot(first_members, second_members, first_static, second_static, groups):
    return jnp.sum(first_members * second_members) + jnp.sum(first_static * second_static) / groups


def shards(ensemble, member_weight, member_of_slot, halfwidth, static_root, innovation, precision):
    member_count = member_weight.shape[0]
    picker = (member_of_slot[:, None] == jnp.arange(member_count, dtype=jnp.int32)[None, :]).astype(
        jnp.float32
    )
    scaled = jnp.sum(picker * member_weight[None, :], axis=1)
    taper = taper_weights(halfwidth, HMAX)
    precise = precision.astype(jnp.float32)
    groups = lax.axis_size("member")
    level_share = precision.shape[0] // groups
    first_level = lax.axis_index("member") * level_share

    def adjoint(weighted):
        folded = scaled[:, None, None, None] * jnp.sum(
            ensemble.astype(jnp.float32) * weighted[None], axis=1
        )
        grad_members = ensemble_share * localize(folded, taper)
        grad_static = static_share * jnp.einsum(
            "ql,qyx->lyx", static_root, jnp.sum(weighted, axis=0), precision=lax.Precision.HIGHEST
        )
        return (grad_members, grad_static)

    res_members, res_static = adjoint(precise[None] * innovation.astype(jnp.float32))
    dir_members, dir_static = (res_members, res_static)
    sol_members = jnp.zeros_like(res_members)
    sol_static = jnp.zeros_like(res_static)
    increment = jnp.zeros((), jnp.float32)
    norm_now = lax.psum(
        local_dot(res_members, res_members, res_static, res_static, groups), ("member", "band")
    )
    for iteration in range(ITERS):
        localized = localize(dir_members, taper)
        partial_image = ensemble_share * jnp.sum(
            scaled[:, None, None, None, None] * ensemble.astype(jnp.float32) * localized[:, None],
            axis=0,
        )
        summed = lax.psum(partial_image, "member")
        static = jnp.einsum("lq,qyx->lyx", static_root, dir_static, precision=lax.Precision.HIGHEST)
        image = summed + static_share * static[None]
        hessian_weighted = precise[None] * image
        hessian_grad_members, hessian_grad_static = adjoint(hessian_weighted)
        hes_members, hes_static, image = (
            dir_members + hessian_grad_members,
            dir_static + hessian_grad_static,
            image,
        )
        curvature = lax.psum(
            local_dot(dir_members, hes_members, dir_static, hes_static, groups), ("member", "band")
        )
        alpha = norm_now / curvature
        sol_members = sol_members + alpha * dir_members
        sol_static = sol_static + alpha * dir_static
        increment = increment + alpha * image
        res_members = res_members - alpha * hes_members
        res_static = res_static - alpha * hes_static
        if iteration + 1 < ITERS:
            norm_next = lax.psum(
                local_dot(res_members, res_members, res_static, res_static, groups),
                ("member", "band"),
            )
            ratio = norm_next / norm_now
            dir_members = res_members + ratio * dir_members
            dir_static = res_static + ratio * dir_static
            norm_now = norm_next
    increment = lax.dynamic_slice_in_dim(increment, first_level, level_share, 1)
    return (sol_members, sol_static, increment)


def solution(mesh):
    return jax.shard_map(
        shards,
        mesh=mesh,
        in_specs=(
            P("member", None, None, "band", None),
            P(),
            P("member"),
            P(),
            P(),
            P(None, None, "band", None),
            P(None, "band", None),
        ),
        out_specs=(
            P("member", None, "band", None),
            P(None, "band", None),
            P(None, "member", "band", None),
        ),
        check_vma=False,
    )
```

profile of v0, /device:TPU:1, one launch (start us, length us, event | category | flops | bytes accessed | tf_op | source)
XLA Modules:
  0.0 658.5 jit_solution(16516160532751708579)
XLA Ops:
  7.2 1.0 convert_element_type.373
  8.9 1.3 fusion.100
  10.1 1.6 fusion.13
  12.9 0.9 convolution_convert_fusion.4
  14.2 4.0 collective-permute-start
  18.2 1.3 collective-permute-start.1
  19.6 1.1 collective-permute-done
  20.8 3.8 collective-permute-done.1
  25.4 0.9 convolution_convert_fusion.3
  26.7 4.0 collective-permute-start.2
  31.0 1.3 collective-permute-start.3
  32.3 1.0 collective-permute-done.2
  33.3 4.1 collective-permute-done.3
  38.1 1.8 fusion.10
  41.3 126.7 %all-reduce.4.cloned.1.call-done = f32[2,16,4,1440]{3,2,1,0:T(4,128)} async-done(((f32[2,16,4,1440]{3,2,1,0:T(4,128)}), f32[2,16,4,1440]{3,2,1,0:T(4,128)}) %all-reduce.4.cloned.1.call-update) | async-done | bytes 737296 | tf_op jit(solution)/shard_map/psum | solution.py:107
  168.0 1.7 multiply_reduce_fusion.1
  171.3 0.9 convolution_convert_fusion.2
  172.6 3.1 collective-permute-start.4
  175.7 1.3 collective-permute-start.5
  177.0 1.4 fusion.42
  179.7 3.3 collective-permute-done.5
  183.0 0.9 constant_dynamic-update-slice_fusion.10
  184.0 2.1 multiply_reduce_fusion.4
  187.4 101.5 %all-reduce = (f32[]{:T(128)}, f32[]{:T(128)}) all-reduce(f32[]{:T(128)S(6)} %add.217, f32[]{:T(128)S(6)} %add.238), channel_id=1, replica_groups=mesh['member'=16,'band'=32] {'member','band'}, use_global_device_ids=true, to_apply=%region_5.6 | all-reduce | flops 2 | bytes 16 | tf_op jit(solution)/shard_map/psum | solution.py:98
  292.7 94.9 %psum.45 = f32[]{:T(128)} all-reduce(f32[]{:T(128)S(6)} %add.239), channel_id=1, replica_groups=mesh['member'=16,'band'=32] {'member','band'}, use_global_device_ids=true, to_apply=%region_14.15 | all-reduce | flops 1 | bytes 8 | tf_op jit(solution)/shard_map/psum | solution.py:127
  389.7 1.2 reshape.309
  391.0 0.9 convolution_convert_fusion.1
  391.9 0.9 copy.131
  392.8 1.2 convert_element_type.417
  394.0 3.7 collective-permute-start.6
  397.7 1.3 collective-permute-start.7
  399.0 2.2 collective-permute-done.6
  401.3 3.8 collective-permute-done.7
  405.8 1.8 fusion.12
  408.1 1.0 copy.133
  409.1 116.4 %all-reduce.6.cloned.1.call-done = f32[2,16,4,1440]{3,2,1,0:T(4,128)} async-done(((f32[2,16,4,1440]{3,2,1,0:T(4,128)}), f32[2,16,4,1440]{3,2,1,0:T(4,128)}) %all-reduce.6.cloned.1.call-update) | async-done | bytes 737296 | tf_op jit(solution)/shard_map/psum | solution.py:107
  525.5 1.8 multiply_reduce_fusion
  529.9 0.9 convolution_convert_fusion
  531.2 3.1 collective-permute-start.8
  534.3 1.3 collective-permute-start.9
  535.6 1.2 fusion.17
  537.8 3.9 collective-permute-done.9
  541.6 0.9 constant_dynamic-update-slice_fusion.18
  542.7 2.0 fusion.39
  545.3 101.3 %psum.47 = f32[]{:T(128)} all-reduce(f32[]{:T(128)S(6)} %add.262), channel_id=1, replica_groups=mesh['member'=16,'band'=32] {'member','band'}, use_global_device_ids=true, to_apply=%region_20.21 | all-reduce | flops 1 | bytes 8 | tf_op jit(solution)/shard_map/psum | solution.py:117
  647.9 1.4 fusion.92
  649.5 1.0 copy.144
  650.6 1.0 copy.143
  (129 shorter events, 14.1 us)
Async XLA Ops:
  7.2 32.8 %copy-start = (f32[16,16]{1,0:T(8,128)S(1)}, f32[16,16]{1,0:T(8,128)}, u32[]{:S(2)}) copy-start(f32[16,16]{1,0:T(8,128)} %param.11) | copy-start | bytes 3076
  7.2 3.0 copy-start.1
  7.2 160.8 %all-reduce.4.cloned.1.call-start = ((), (), s32[]{:S(2)}) async-start(), calls=%async_computation | async-start | bytes 1572864 | tf_op jit(solution)/shard_map/psum | solution.py:107
  12.9 158.4 %copy-start.25 = (s32[516]{0:T(1024)}, s32[516]{0:T(1024)S(1)}, u32[]{:S(2)}) copy-start(s32[516]{0:T(1024)S(1)} %iota_add_fusion) | copy-start | bytes 6196
  13.8 5.7 copy-start.28
  14.2 6.6 collective-permute-start
  18.2 6.4 collective-permute-start.1
  19.6 17.9 %copy-start.4 = (f32[16]{0:T(128)}, f32[16]{0:T(128)S(1)}, u32[]{:S(2)}) copy-start(f32[16]{0:T(128)S(1)} %get-tuple-element.60) | copy-start | bytes 196
  19.6 17.9 %copy-start.7 = (f32[16]{0:T(128)}, f32[16]{0:T(128)S(1)}, u32[]{:S(2)}) copy-start(f32[16]{0:T(128)S(1)} %get-tuple-element.61) | copy-start | bytes 196
  19.6 17.9 %copy-start.10 = (f32[16]{0:T(128)}, f32[16]{0:T(128)S(1)}, u32[]{:S(2)}) copy-start(f32[16]{0:T(128)S(1)} %get-tuple-element.62) | copy-start | bytes 196
  19.6 17.9 %copy-start.13 = (f32[16]{0:T(128)}, f32[16]{0:T(128)S(1)}, u32[]{:S(2)}) copy-start(f32[16]{0:T(128)S(1)} %get-tuple-element.63) | copy-start | bytes 196
  19.6 17.9 %copy-start.16 = (f32[16]{0:T(128)}, f32[16]{0:T(128)S(1)}, u32[]{:S(2)}) copy-start(f32[16]{0:T(128)S(1)} %get-tuple-element.64) | copy-start | bytes 196
  19.6 17.9 %copy-start.19 = (f32[16]{0:T(128)}, f32[16]{0:T(128)S(1)}, u32[]{:S(2)}) copy-start(f32[16]{0:T(128)S(1)} %get-tuple-element.65) | copy-start | bytes 196
  19.6 17.9 %copy-start.22 = (f32[16]{0:T(128)}, f32[16]{0:T(128)S(1)}, u32[]{:S(2)}) copy-start(f32[16]{0:T(128)S(1)} %get-tuple-element.66) | copy-start | bytes 196
  26.2 4.5 copy-start.3
  26.7 6.6 %collective-permute-start.2 = (bf16[1,16,4,1440]{3,1,2,0:T(8,128)(2,1)S(1)}, bf16[1,16,4,1440]{3,1,2,0:T(8,128)(2,1)S(1)}, u32[]{:S(2)}, u32[]{:S(2)}) collective-permute-start(bf16[1,16,4,1440]{3,1,2,0:T(8,128)(2,1)S(1)} %convert_element_type.392), channel_id=1, source_target_pairs={{0,1},{1,2},{2,3},{3,4},{4,5},{5,6},{6,7},{7,8},{8,9},{9,10},{10,1... | collective-permute-start | bytes 552968 | tf_op jit(solution)/shard_map/ppermute | solution.py:20
  31.0 6.4 collective-permute-start.3
  39.9 485.6 %all-reduce.6.cloned.1.call-start = ((), (), s32[]{:S(2)}) async-start(), calls=%async_computation.1 | async-start | bytes 1572864 | tf_op jit(solution)/shard_map/psum | solution.py:107
  172.6 7.1 %collective-permute-start.4 = (bf16[1,16,4,1440]{3,1,2,0:T(8,128)(2,1)S(1)}, bf16[1,16,4,1440]{3,1,2,0:T(8,128)(2,1)S(1)}, u32[]{:S(2)}, u32[]{:S(2)}) collective-permute-start(bf16[1,16,4,1440]{3,1,2,0:T(8,128)(2,1)S(1)} %convert_element_type.405), channel_id=1, source_target_pairs={{0,1},{1,2},{2,3},{3,4},{4,5},{5,6},{6,7},{7,8},{8,9},{9,10},{10,1... | collective-permute-start | bytes 552968 | tf_op jit(solution)/shard_map/ppermute | solution.py:20
  175.7 7.3 %collective-permute-start.5 = (bf16[1,16,4,1440]{3,1,2,0:T(8,128)(2,1)S(1)}, bf16[1,16,4,1440]{3,1,2,0:T(8,128)(2,1)}, u32[]{:S(2)}, u32[]{:S(2)}) collective-permute-start(bf16[1,16,4,1440]{3,1,2,0:T(8,128)(2,1)S(1)} %convert_element_type.405), channel_id=1, source_target_pairs={{1,0},{2,1},{3,2},{4,3},{5,4},{6,5},{7,6},{8,7},{9,8},{10,9},{11,1... | collective-permute-start | bytes 552968 | tf_op jit(solution)/shard_map/ppermute | solution.py:23
  389.7 1.3 copy-start.26
  394.0 11.1 %copy-start.5 = (f32[16]{0:T(128)S(1)}, f32[16]{0:T(128)}, u32[]{:S(2)}) copy-start(f32[16]{0:T(128)} %copy-done.4) | copy-start | bytes 196
  394.0 11.1 %copy-start.8 = (f32[16]{0:T(128)S(1)}, f32[16]{0:T(128)}, u32[]{:S(2)}) copy-start(f32[16]{0:T(128)} %copy-done.7) | copy-start | bytes 196
  394.0 11.1 %copy-start.11 = (f32[16]{0:T(128)S(1)}, f32[16]{0:T(128)}, u32[]{:S(2)}) copy-start(f32[16]{0:T(128)} %copy-done.10) | copy-start | bytes 196
  394.0 11.1 %copy-start.14 = (f32[16]{0:T(128)S(1)}, f32[16]{0:T(128)}, u32[]{:S(2)}) copy-start(f32[16]{0:T(128)} %copy-done.13) | copy-start | bytes 196
  394.0 11.1 %copy-start.17 = (f32[16]{0:T(128)S(1)}, f32[16]{0:T(128)}, u32[]{:S(2)}) copy-start(f32[16]{0:T(128)} %copy-done.16) | copy-start | bytes 196
  394.0 11.1 %copy-start.20 = (f32[16]{0:T(128)S(1)}, f32[16]{0:T(128)}, u32[]{:S(2)}) copy-start(f32[16]{0:T(128)} %copy-done.19) | copy-start | bytes 196
  394.0 11.1 %copy-start.23 = (f32[16]{0:T(128)S(1)}, f32[16]{0:T(128)}, u32[]{:S(2)}) copy-start(f32[16]{0:T(128)} %copy-done.22) | copy-start | bytes 196
  394.0 7.2 %collective-permute-start.6 = (bf16[1,16,4,1440]{3,1,2,0:T(8,128)(2,1)S(1)}, bf16[1,16,4,1440]{3,1,2,0:T(8,128)(2,1)S(1)}, u32[]{:S(2)}, u32[]{:S(2)}) collective-permute-start(bf16[1,16,4,1440]{3,1,2,0:T(8,128)(2,1)S(1)} %convert_element_type.417), channel_id=1, source_target_pairs={{0,1},{1,2},{2,3},{3,4},{4,5},{5,6},{6,7},{7,8},{8,9},{9,10},{10,1... | collective-permute-start | bytes 552968 | tf_op jit(solution)/shard_map/ppermute | solution.py:20
  397.7 7.4 %collective-permute-start.7 = (bf16[1,16,4,1440]{3,1,2,0:T(8,128)(2,1)S(1)}, bf16[1,16,4,1440]{3,1,2,0:T(8,128)(2,1)S(1)}, u32[]{:S(2)}, u32[]{:S(2)}) collective-permute-start(bf16[1,16,4,1440]{3,1,2,0:T(8,128)(2,1)S(1)} %convert_element_type.417), channel_id=1, source_target_pairs={{1,0},{2,1},{3,2},{4,3},{5,4},{6,5},{7,6},{8,7},{9,8},{10,9},{11,1... | collective-permute-start | bytes 552968 | tf_op jit(solution)/shard_map/ppermute | solution.py:23
  527.3 0.9 copy-start.2
  529.2 0.7 copy-start.27
  531.2 6.5 collective-permute-start.8
  534.3 7.3 %collective-permute-start.9 = (bf16[1,16,4,1440]{3,1,2,0:T(8,128)(2,1)S(1)}, bf16[1,16,4,1440]{3,1,2,0:T(8,128)(2,1)}, u32[]{:S(2)}, u32[]{:S(2)}) collective-permute-start(bf16[1,16,4,1440]{3,1,2,0:T(8,128)(2,1)S(1)} %convert_element_type.430), channel_id=1, source_target_pairs={{1,0},{2,1},{3,2},{4,3},{5,4},{6,5},{7,6},{8,7},{9,8},{10,9},{11,1... | collective-permute-start | bytes 552968 | tf_op jit(solution)/shard_map/ppermute | solution.py:23
  536.8 5.7 copy-start.6
  536.8 5.8 copy-start.9
  536.8 5.8 copy-start.12
  536.9 5.8 copy-start.15
  536.9 5.8 copy-start.18
  536.9 5.8 copy-start.21
  536.9 5.8 copy-start.24
Sparse Core Ops, SparseCore 0:
  40.1 127.9 all-reduce.3
  407.7 117.7 all-reduce.5
where the time goes:
time: 659 us; the launch traced here: 658 us
  blocking collectives  298 us (45%)
  waiting for transfers between devices  266 us (40%)
  between operations  24.5 us (4%)
  starting transfers between devices  24.4 us (4%)
  other arithmetic  23.4 us (4%)
  local copies, waits for them, and re-layouts  13.4 us (2%)
  matrix products  8.49 us (1%)
    psum x2, waiting for transfers between devices, shards(): summed = lax.psum(partial_image, 'member')  243 us
    psum x2, blocking collectives, shards(): lax.psum(local_dot(res_members, res_members, res_static, res_static, grou...  196 us
    psum x1, blocking collectives, shards(): lax.psum(local_dot(dir_members, hes_members, dir_static, hes_static, grou...  101 us
    ppermute x5, waiting for transfers between devices, with_halo(): lax.ppermute(lax.slice_in_dim(block, 0, width, axis=dim), axis, backward)  18.7 us
    ppermute x5, starting transfers between devices, with_halo(): lax.ppermute(lax.slice_in_dim(block, block.shape[dim] - width, None, axis...  17.9 us
  transfers between devices with their start and end apart: 12, of which 11 were waited for; matrix products, arithmetic and copies ran while one was open for 1% of the time, Pallas kernels for 0%

commit v1 on v0

--- a/solution.py
+++ b/solution.py
@@ -95,9 +95,9 @@
     sol_members = jnp.zeros_like(res_members)
     sol_static = jnp.zeros_like(res_static)
     increment = jnp.zeros((), jnp.float32)
-    norm_now = lax.psum(
-        local_dot(res_members, res_members, res_static, res_static, groups), ("member", "band")
-    )
+    norm_now = local_dot(res_members, res_members, res_static, res_static, groups)
+    for mesh_axis in ("member", "band"):
+        norm_now = lax.psum(norm_now, mesh_axis)
     for iteration in range(ITERS):
         localized = localize(dir_members, taper)
         partial_image = ensemble_share * jnp.sum(

time: 659 us -> 754 us (1.14)
  blocking collectives: 298 us -> 392 us
    psum x1 -> x2, blocking collectives: 101 us -> 202 us  [shards(): lax.psum(local_dot(dir_members, hes_members, dir_static, hes_static, grou...]
    psum x2 -> x1, blocking collectives: 196 us -> 108 us  [shards(): lax.psum(local_dot(res_members, res_members, res_static, res_static, grou...]
    psum x0 -> x2, blocking collectives: none -> 82.3 us  [shards(): norm_now = lax.psum(norm_now, mesh_axis)]
where the time goes in v1:
time: 754 us; the launch traced here: 753 us
  blocking collectives  392 us (52%)
  waiting for transfers between devices  267 us (35%)
  between operations  24.5 us (3%)
  starting transfers between devices  24.4 us (3%)
  other arithmetic  23.3 us (3%)
  local copies, waits for them, and re-layouts  13.4 us (2%)
  matrix products  8.45 us (1%)
    psum x2, waiting for transfers between devices, shards(): summed = lax.psum(partial_image, 'member')  243 us
    psum x2, blocking collectives, shards(): lax.psum(local_dot(dir_members, hes_members, dir_static, hes_static, grou...  202 us
    psum x1, blocking collectives, shards(): lax.psum(local_dot(res_members, res_members, res_static, res_static, grou...  108 us
    psum x2, blocking collectives, shards(): norm_now = lax.psum(norm_now, mesh_axis)  82.3 us
    ppermute x5, waiting for transfers between devices, with_halo(): lax.ppermute(lax.slice_in_dim(block, 0, width, axis=dim), axis, backward)  18.8 us
    ppermute x5, starting transfers between devices, with_halo(): lax.ppermute(lax.slice_in_dim(block, block.shape[dim] - width, None, axis...  17.9 us
  transfers between devices with their start and end apart: 12, of which 11 were waited for; matrix products, arithmetic and copies ran while one was open for 1% of the time, Pallas kernels for 0%

profile of v1, /device:TPU:1, one launch (start us, length us, event | category | flops | bytes accessed | tf_op | source)
XLA Modules:
  0.0 753.2 jit_solution(16499442976550567291)
XLA Ops:
  7.2 1.0 convert_element_type.373
  8.9 1.3 fusion.100
  10.1 1.6 fusion.13
  14.2 4.0 collective-permute-start
  18.2 1.3 collective-permute-start.1
  19.6 1.1 collective-permute-done
  20.8 3.8 collective-permute-done.1
  25.4 0.9 convolution_convert_fusion.3
  26.7 4.0 collective-permute-start.2
  31.0 1.3 collective-permute-start.3
  32.3 1.0 collective-permute-done.2
  33.3 4.1 collective-permute-done.3
  38.1 1.8 fusion.10
  41.3 126.7 %all-reduce.3.cloned.1.call-done = f32[2,16,4,1440]{3,2,1,0:T(4,128)} async-done(((f32[2,16,4,1440]{3,2,1,0:T(4,128)}), f32[2,16,4,1440]{3,2,1,0:T(4,128)}) %all-reduce.3.cloned.1.call-update) | async-done | bytes 737296 | tf_op jit(solution)/shard_map/psum | solution.py:107
  168.0 1.7 multiply_reduce_fusion.1
  172.6 3.1 collective-permute-start.4
  175.7 1.3 collective-permute-start.5
  177.0 1.3 fusion.42
  179.6 3.4 collective-permute-done.5
  183.0 0.9 constant_dynamic-update-slice_fusion.10
  184.0 2.0 multiply_reduce_fusion.4
  187.3 25.4 %psum.49 = f32[]{:T(128)} all-reduce(f32[]{:T(128)S(6)} %add.219), channel_id=1, replica_groups=mesh['member'=16,'band'=32] {'member'}, use_global_device_ids=true, to_apply=%region_5.6 | all-reduce | flops 1 | bytes 8 | tf_op jit(solution)/shard_map/psum | solution.py:100
  212.7 100.4 %psum.52 = f32[]{:T(128)} all-reduce(f32[]{:T(128)S(6)} %add.240), channel_id=1, replica_groups=mesh['member'=16,'band'=32] {'member','band'}, use_global_device_ids=true, to_apply=%region_12.13 | all-reduce | flops 1 | bytes 8 | tf_op jit(solution)/shard_map/psum | solution.py:117
  313.1 56.9 %psum.50 = f32[]{:T(128)} all-reduce(f32[]{:T(128)} %psum.49), channel_id=1, replica_groups=mesh['member'=16,'band'=32] {'band'}, use_global_device_ids=true, to_apply=%region_6.7 | all-reduce | flops 1 | bytes 8 | tf_op jit(solution)/shard_map/psum | solution.py:100
  373.8 108.2 %psum.53 = f32[]{:T(128)} all-reduce(f32[]{:T(128)S(6)} %add.241), channel_id=1, replica_groups=mesh['member'=16,'band'=32] {'member','band'}, use_global_device_ids=true, to_apply=%region_15.16 | all-reduce | flops 1 | bytes 8 | tf_op jit(solution)/shard_map/psum | solution.py:127
  484.1 1.2 reshape.309
  485.4 0.9 convolution_convert_fusion.1
  486.3 0.9 copy.131
  487.2 1.2 convert_element_type.417
  488.4 3.7 collective-permute-start.6
  492.1 1.3 collective-permute-start.7
  493.4 2.3 collective-permute-done.6
  495.7 3.8 collective-permute-done.7
  500.2 1.8 fusion.12
  502.5 1.0 copy.133
  503.5 116.7 %all-reduce.5.cloned.1.call-done = f32[2,16,4,1440]{3,2,1,0:T(4,128)} async-done(((f32[2,16,4,1440]{3,2,1,0:T(4,128)}), f32[2,16,4,1440]{3,2,1,0:T(4,128)}) %all-reduce.5.cloned.1.call-update) | async-done | bytes 737296 | tf_op jit(solution)/shard_map/psum | solution.py:107
  620.2 1.8 multiply_reduce_fusion
  624.6 0.9 convolution_convert_fusion
  625.9 3.1 collective-permute-start.8
  629.0 1.3 collective-permute-start.9
  630.3 1.2 fusion.17
  632.5 3.9 collective-permute-done.9
  636.4 0.9 constant_dynamic-update-slice_fusion.18
  637.4 2.0 fusion.39
  640.0 101.3 %psum.55 = f32[]{:T(128)} all-reduce(f32[]{:T(128)S(6)} %add.264), channel_id=1, replica_groups=mesh['member'=16,'band'=32] {'member','band'}, use_global_device_ids=true, to_apply=%region_21.22 | all-reduce | flops 1 | bytes 8 | tf_op jit(solution)/shard_map/psum | solution.py:117
  742.7 1.4 fusion.92
  744.3 1.0 copy.144
  745.4 1.0 copy.143
  (131 shorter events, 15.9 us)
Async XLA Ops:
  7.2 32.8 %copy-start = (f32[16,16]{1,0:T(8,128)S(1)}, f32[16,16]{1,0:T(8,128)}, u32[]{:S(2)}) copy-start(f32[16,16]{1,0:T(8,128)} %param.11) | copy-start | bytes 3076
  7.2 3.0 copy-start.1
  7.2 160.8 %all-reduce.3.cloned.1.call-start = ((), (), s32[]{:S(2)}) async-start(), calls=%async_computation | async-start | bytes 1572864 | tf_op jit(solution)/shard_map/psum | solution.py:107
  12.9 158.4 %copy-start.25 = (s32[516]{0:T(1024)}, s32[516]{0:T(1024)S(1)}, u32[]{:S(2)}) copy-start(s32[516]{0:T(1024)S(1)} %iota_add_fusion) | copy-start | bytes 6196
  13.8 5.7 copy-start.28
  14.2 6.6 collective-permute-start
  18.2 6.4 collective-permute-start.1
  19.6 17.9 %copy-start.4 = (f32[16]{0:T(128)}, f32[16]{0:T(128)S(1)}, u32[]{:S(2)}) copy-start(f32[16]{0:T(128)S(1)} %get-tuple-element.58) | copy-start | bytes 196
  19.6 17.9 %copy-start.7 = (f32[16]{0:T(128)}, f32[16]{0:T(128)S(1)}, u32[]{:S(2)}) copy-start(f32[16]{0:T(128)S(1)} %get-tuple-element.59) | copy-start | bytes 196
  19.6 17.9 %copy-start.10 = (f32[16]{0:T(128)}, f32[16]{0:T(128)S(1)}, u32[]{:S(2)}) copy-start(f32[16]{0:T(128)S(1)} %get-tuple-element.60) | copy-start | bytes 196
  19.6 17.9 %copy-start.13 = (f32[16]{0:T(128)}, f32[16]{0:T(128)S(1)}, u32[]{:S(2)}) copy-start(f32[16]{0:T(128)S(1)} %get-tuple-element.61) | copy-start | bytes 196
  19.6 17.9 %copy-start.16 = (f32[16]{0:T(128)}, f32[16]{0:T(128)S(1)}, u32[]{:S(2)}) copy-start(f32[16]{0:T(128)S(1)} %get-tuple-element.62) | copy-start | bytes 196
  19.6 17.9 %copy-start.19 = (f32[16]{0:T(128)}, f32[16]{0:T(128)S(1)}, u32[]{:S(2)}) copy-start(f32[16]{0:T(128)S(1)} %get-tuple-element.63) | copy-start | bytes 196
  19.6 17.9 %copy-start.22 = (f32[16]{0:T(128)}, f32[16]{0:T(128)S(1)}, u32[]{:S(2)}) copy-start(f32[16]{0:T(128)S(1)} %get-tuple-element.64) | copy-start | bytes 196
  26.2 4.5 copy-start.3
  26.7 6.6 collective-permute-start.2
  31.0 6.4 collective-permute-start.3
  39.9 580.3 %all-reduce.5.cloned.1.call-start = ((), (), s32[]{:S(2)}) async-start(), calls=%async_computation.1 | async-start | bytes 1572864 | tf_op jit(solution)/shard_map/psum | solution.py:107
  172.6 7.0 collective-permute-start.4
  175.7 7.3 collective-permute-start.5
  484.1 1.3 copy-start.26
  488.3 11.1 %copy-start.5 = (f32[16]{0:T(128)S(1)}, f32[16]{0:T(128)}, u32[]{:S(2)}) copy-start(f32[16]{0:T(128)} %copy-done.4) | copy-start | bytes 196
  488.3 11.1 %copy-start.8 = (f32[16]{0:T(128)S(1)}, f32[16]{0:T(128)}, u32[]{:S(2)}) copy-start(f32[16]{0:T(128)} %copy-done.7) | copy-start | bytes 196
  488.3 11.1 %copy-start.11 = (f32[16]{0:T(128)S(1)}, f32[16]{0:T(128)}, u32[]{:S(2)}) copy-start(f32[16]{0:T(128)} %copy-done.10) | copy-start | bytes 196
  488.4 11.1 %copy-start.14 = (f32[16]{0:T(128)S(1)}, f32[16]{0:T(128)}, u32[]{:S(2)}) copy-start(f32[16]{0:T(128)} %copy-done.13) | copy-start | bytes 196
  488.4 11.1 %copy-start.17 = (f32[16]{0:T(128)S(1)}, f32[16]{0:T(128)}, u32[]{:S(2)}) copy-start(f32[16]{0:T(128)} %copy-done.16) | copy-start | bytes 196
  488.4 11.1 %copy-start.20 = (f32[16]{0:T(128)S(1)}, f32[16]{0:T(128)}, u32[]{:S(2)}) copy-start(f32[16]{0:T(128)} %copy-done.19) | copy-start | bytes 196
  488.4 11.1 %copy-start.23 = (f32[16]{0:T(128)S(1)}, f32[16]{0:T(128)}, u32[]{:S(2)}) copy-start(f32[16]{0:T(128)} %copy-done.22) | copy-start | bytes 196
  488.4 7.3 collective-permute-start.6
  492.1 7.4 collective-permute-start.7
  622.0 0.9 copy-start.2
  623.9 0.7 copy-start.27
  625.9 6.5 collective-permute-start.8
  629.0 7.3 collective-permute-start.9
  631.6 5.7 copy-start.6
  631.6 5.7 copy-start.9
  631.6 5.8 copy-start.12
  631.6 5.8 copy-start.15
  631.6 5.8 copy-start.18
  631.6 5.8 copy-start.21
  631.6 5.8 copy-start.24
Sparse Core Ops, SparseCore 0:
  40.1 127.9 all-reduce.2
  502.1 118.0 all-reduce.4
